TPU v7x, 32 devices: a whole 2x2x4 slice. The times are simulated.
32 devices in a mesh: section: 4 (over y, x), ctx: 8 (over z, core).
Axes of the slice: x: 2, y: 2, z: 4, core: 2. Of those that a mesh axis runs over, the one named last changes fastest.
Arguments:
- resid: bfloat16 [4, 1024, 6144], P('section', 'ctx'), may hold values from -6 to 6
- queries: bfloat16 [4, 1024, 6144], P('section', 'ctx'), may hold values from -6 to 6
- keys: bfloat16 [4, 1024, 6144], P('section', 'ctx'), may hold values from -6 to 6
- values: bfloat16 [4, 1024, 6144], P('section', 'ctx'), may hold values from -6 to 6
- log_decay: float32 [4, 1024, 48], P('section', 'ctx'), may hold values from -3 to 0
- attn_gain: float32 [4, 6144], P('section'), may hold values from 0.25 to 1.75
- moe_gain: float32 [4, 6144], P('section'), may hold values from 0.25 to 1.75
- experts: int32 [4, 1024, 2], P('section', 'ctx'), may hold values from 0 to 31, all different within a row; in each aligned block of 128 rows (0 to 127, 128 to 255, ..., all dimensions but the last counted through in order) at most 16 rows name the same one
- combine_weight: float32 [4, 1024, 2], P('section', 'ctx'), may hold values from 0.2 to 1
- w_up: bfloat16 [4, 6144, 5120], P('section', None, 'ctx'), may hold values from -0.078125 to 0.078125
- w_down: bfloat16 [4, 5120, 6144], P('section', 'ctx'), may hold values from -0.078125 to 0.078125
Outputs:
- received: bfloat16 [4, 1024, 6144], P('section', 'ctx')
Inputs may be any that keep to these rules, and one draw needn't show every extreme that they name: In the rows of one device each expert is named at most 16 times, and the two experts of a token differ.
All inputs are finite; a program needn't handle non-finite values.
Results may differ from a plain program's by a relative error of at most 0.002.
Values may be sent and summed in bfloat16 or wider, within the bound.
No kernel may reach another device: no remote copies, remote signals or barrier semaphores. Data moves between devices by JAX's collectives and lax.ppermute only.
A program may use at most 256 MiB of HBM per device.

v0:
```python
import jax
import jax.numpy as jnp
from jax import lax
from jax.sharding import PartitionSpec as P

D = 6144
LINEAR_HEADS = 48
HEAD = 128
EXPERTS = 32
SHARDS = 8
CAP_SRC = 16
HIGH = lax.Precision.HIGHEST


def prefix_2(part, axis, combine, identity):
    place = lax.axis_index(axis)
    gathered = jax.tree.map(lambda a: lax.all_gather(a, axis), part)
    state = jax.tree.map(lambda a, e: jnp.zeros_like(a) + jnp.asarray(e, a.dtype), part, identity)

    def one(step, state):
        return combine(
            state, jax.tree.map(lambda a: lax.dynamic_index_in_dim(a, step, 0, False), gathered)
        )

    return lax.fori_loop(0, place, one, state)


def passed_along(value, axis, steps):
    count = lax.axis_size(axis)
    pairs = [(source, (source + steps) % count) for source in range(count)]
    return lax.ppermute(value, axis, pairs)


def rms_scale(values_in, gain):
    return (
        values_in
        * lax.rsqrt(jnp.mean(values_in * values_in, axis=-1, keepdims=True) + 1e-06)
        * gain
    )


def slots_of(chosen):
    onehot = (chosen[:, None] == jnp.arange(EXPERTS)[None, :]).astype(jnp.int32)
    before = jnp.cumsum(onehot, axis=0) - onehot
    return jnp.sum(before * onehot, axis=1)


def join_states(earlier, later):
    return (earlier[0] * later[0], later[0][:, None, None] * earlier[1] + later[1])


def local(
    resid,
    queries,
    keys,
    values,
    log_decay,
    attn_gain,
    moe_gain,
    experts,
    combine_weight,
    w_up,
    w_down,
):
    length = queries.shape[1]
    query = queries[0].astype(jnp.float32).reshape(length, LINEAR_HEADS, HEAD)
    keyrows = keys[0].astype(jnp.float32).reshape(length, LINEAR_HEADS, HEAD)
    valrows = values[0].astype(jnp.float32).reshape(length, LINEAR_HEADS, HEAD)
    log_rate = log_decay[0]
    cumul = jnp.cumsum(log_rate, axis=0)
    scores = jnp.einsum("thd,shd->hts", query, keyrows, precision=HIGH)
    spread = cumul.T[:, :, None] - cumul.T[:, None, :]
    lower = jnp.arange(length)[:, None] >= jnp.arange(length)[None, :]
    weights = jnp.exp(jnp.where(lower[None], spread, -1e30))
    intra = jnp.einsum("hts,shd->thd", scores * weights, valrows, precision=HIGH)
    tail_decay = jnp.exp(cumul[-1][None, :] - cumul)
    state = jnp.einsum("thd,the->hde", keyrows * tail_decay[:, :, None], valrows, precision=HIGH)
    identity = (
        jnp.ones((LINEAR_HEADS,), jnp.float32),
        jnp.zeros((LINEAR_HEADS, HEAD, HEAD), jnp.float32),
    )
    prefix = prefix_2((jnp.exp(cumul[-1]), state), "ctx", join_states, identity)
    inter = jnp.exp(cumul)[:, :, None] * jnp.einsum(
        "thd,hde->the", query, prefix[1], precision=HIGH
    )
    attn_raw = (intra + inter).reshape(length, D)
    hres = resid[0].astype(jnp.float32) + rms_scale(attn_raw, attn_gain[0])
    normed = rms_scale(hres, moe_gain[0]).astype(jnp.bfloat16)
    ctx_count = lax.axis_size("ctx")
    flying = ctx_count // SHARDS
    my_expert = lax.axis_index("ctx") // SHARDS
    chosen = experts[0].reshape(-1)
    slot = slots_of(chosen)
    target = chosen * CAP_SRC + slot
    in_window = chosen < flying
    select = (
        (target[None, :] == jnp.arange(flying * CAP_SRC)[:, None]) & in_window[None, :]
    ).astype(jnp.bfloat16)
    doubled = jnp.repeat(normed, 2, axis=0)
    outbox = jnp.dot(select, doubled, preferred_element_type=jnp.float32).astype(jnp.bfloat16)
    outbox = outbox.reshape(flying, CAP_SRC, D)
    up_local = w_up[0]
    down_local = w_down[0]
    mine = lax.dynamic_index_in_dim(
        lax.all_gather(outbox[None], "ctx", axis=0, tiled=True), my_expert, 1, False
    )
    count = mine.shape[0]
    hidden = jax.nn.gelu(
        jnp.dot(mine.reshape(count * CAP_SRC, D), up_local, preferred_element_type=jnp.float32),
        approximate=True,
    ).astype(jnp.bfloat16)
    partial_value = (
        jnp.dot(hidden, down_local, preferred_element_type=jnp.float32)
        .astype(jnp.bfloat16)
        .reshape(count, CAP_SRC, D)
    )
    returned = lax.all_to_all(partial_value, "ctx", split_axis=0, concat_axis=0, tiled=True)
    summed = returned.reshape(flying, SHARDS, CAP_SRC, D).astype(jnp.float32).sum(axis=1)
    summed = summed.reshape(flying * CAP_SRC, D)
    picked = jnp.take(summed, jnp.clip(target, 0, flying * CAP_SRC - 1), axis=0)
    picked = jnp.where(in_window[:, None], picked, 0.0) * combine_weight[0].reshape(-1)[:, None]
    mixed = picked.reshape(length, 2, D).sum(axis=1)
    layer_out = (hres + mixed).astype(jnp.bfloat16)
    return passed_along(layer_out[None], "section", 1)


def solution(mesh):
    return jax.shard_map(
        local,
        mesh=mesh,
        in_specs=(
            P("section", "ctx", None),
            P("section", "ctx", None),
            P("section", "ctx", None),
            P("section", "ctx", None),
            P("section", "ctx", None),
            P("section", None),
            P("section", None),
            P("section", "ctx", None),
            P("section", "ctx", None),
            P("section", None, "ctx"),
            P("section", "ctx", None),
        ),
        out_specs=P("section", "ctx", None),
        check_vma=False,
    )
```

profile of v0, /device:TPU:0, one launch (start us, length us, event | category | flops | bytes accessed | tf_op | source)
XLA Modules:
  0.0 450.4 jit_solution(3672909860523334791)
XLA Ops:
  7.8 1.9 copy.66
  10.1 1.2 copy-done.2
  11.3 3.6 fusion.11
  16.1 1.8 copy.68
  18.8 13.5 %all-gather.2 = f32[8,1,48]{2,1,0:T(1,128)S(1)} all-gather(f32[1,1,48]{2,1,0:T(1,128)S(1)} %get-tuple-element.63), channel_id=1, replica_groups=mesh['section'=4,'ctx'=8] {'ctx'}, dimensions={0}, use_global_device_ids=true | all-gather | bytes 1728 | tf_op jit(solution)/shard_map/all_gather | solution.py:17
  34.0 5.5 %fusion.14 = f32[48,128,128]{1,2,0:T(8,128)} fusion(f32[48,128,128]{2,1,0:T(8,128)S(1)} %fusion.27, f32[48,128]{1,0:T(8,128)S(1)} %copy.48, pred[128,128]{1,0:T(8,128)(4,1)S(1)} %iota_compare_fusion, bf16[128,48,128]{2,1,0:T(8,128)(2,1)S(1)} %bitcast.101), kind=kOutput, calls=%fused_computation.24 | convolution fusion | flops 1210318848 | bytes 7905280 | tf_op jit(solution)/shard_map/hts,shd->thd/dot_general | solution.py:75
  39.4 198.3 %all-gather.6.cloned.1.call-done = f32[384,128,128]{2,1,0:T(8,128)} async-done(((f32[48,128,128]{2,1,0:T(8,128)}), f32[384,128,128]{2,1,0:T(8,128)}) %all-gather.6.cloned.1.call-update) | async-done | bytes 25165840 | tf_op jit(solution)/shard_map/all_gather | solution.py:17
  238.3 6.8 %multiply_reduce_fusion.2 = (f32[128]{0:T(128)S(1)}, f32[128,48,128]{0,2,1:T(8,128)}) fusion(f32[48,128,128]{2,1,0:T(8,128)S(1)} %get-tuple-element.49, bf16[128,48,128]{2,1,0:T(8,128)(2,1)} %bitcast.97, f32[128,48]{0,1:T(8,128)S(1)} %copy.51, f32[48,128,128]{1,2,0:T(8,128)} %fusion.14), kind=kOutput, calls=%fused_computation.20 | convolution fusion | flops 1211105152 | bytes 11035136 | tf_op jit(solution)/shard_map/thd,hde->the/dot_general | solution.py:83
  245.1 2.4 copy.63
  247.5 2.3 multiply_reduce_fusion.1
  249.8 1.9 multiply_convert_fusion
  251.7 5.0 %broadcast_in_dim.63 = bf16[128,2,6144]{2,1,0:T(2,128)(2,1)} broadcast(bf16[128,6144]{1,0:T(8,128)(2,1)} %multiply_convert_fusion), dimensions={0,2} | broadcast | bytes 4718592 | tf_op jit(solution)/shard_map/broadcast_in_dim | solution.py:99
  256.7 6.2 %reshape.246 = bf16[256,6144]{1,0:T(8,128)(2,1)S(1)} reshape(bf16[128,2,6144]{2,1,0:T(2,128)(2,1)} %broadcast_in_dim.63) | data formatting | bytes 6291456 | tf_op jit(solution)/shard_map/reshape | solution.py:99
  264.1 40.8 %all-gather.8.cloned.1.call-done = bf16[128,6144]{1,0:T(8,128)(2,1)} async-done(((bf16[16,6144]{1,0:T(8,128)(2,1)}), bf16[128,6144]{1,0:T(8,128)(2,1)}) %all-gather.8.cloned.1.call-update) | async-done | bytes 1572880 | tf_op jit(solution)/shard_map/all_gather | solution.py:105
  304.9 9.8 %fusion.4 = bf16[128,6144]{1,0:T(8,128)(2,1)} fusion(bf16[1,640,6144]{2,1,0:T(8,128)(2,1)} %param.23, bf16[128,6144]{1,0:T(8,128)(2,1)} %all-gather.8.cloned.1.call-done, bf16[1,6144,640]{2,1,0:T(8,128)(2,1)} %param.22), kind=kOutput, calls=%fused_computation.7 | convolution fusion | flops 2014789632 | bytes 18874368 | tf_op jit(solution)/shard_map/dot_general | solution.py:113
  314.7 4.8 %all-to-all-start = ((bf16[8,16,6144]{2,1,0:T(8,128)(2,1)}), bf16[8,16,6144]{2,1,0:T(8,128)(2,1)}, u32[]{:S(2)}, u32[]{:S(2)}) async-start(bf16[8,16,6144]{2,1,0:T(8,128)(2,1)} %bitcast.103), calls=%async_computation | async-start | bytes 3145728 | tf_op jit(solution)/shard_map/all_to_all | solution.py:117
  320.1 2.4 copy.57
  322.5 34.6 %all-to-all-done = bf16[8,16,6144]{2,1,0:T(8,128)(2,1)} async-done(((bf16[8,16,6144]{2,1,0:T(8,128)(2,1)}), bf16[8,16,6144]{2,1,0:T(8,128)(2,1)}, u32[]{:S(2)}, u32[]{:S(2)}) %all-to-all-start) | async-done | bytes 1572896 | tf_op jit(solution)/shard_map/all_to_all | solution.py:117
  357.0 1.7 convert_reduce_fusion
  358.7 5.1 %gather_fusion = f32[256,6144]{1,0:T(8,128)} fusion(f32[16,6144]{1,0:T(8,128)S(1)} %convert_reduce_fusion, s32[1024]{0:T(1024)S(1)} %pad_clamp_fusion), kind=kCustom, calls=%fused_computation | custom fusion | bytes 12583936 | tf_op jit(solution)/shard_map/jit(_take)/gather | solution.py:120
  363.8 8.1 %gather.7 = f32[128,2,6144]{2,1,0:T(2,128)} reshape(f32[256,6144]{1,0:T(8,128)} %gather_fusion) | data formatting | bytes 12582912 | tf_op jit(solution)/shard_map/jit(_take)/gather | solution.py:120
  372.0 32.9 %multiply_reduce_fusion = f32[128,6144]{1,0:T(8,128)S(1)} fusion(f32[128,2,6144]{2,1,0:T(2,128)} %gather.7, pred[128,2]{1,0:T(8,128)(4,1)S(1)} %compare_and_fusion, pred[128,2]{1,0:T(8,128)(4,1)S(1)} %copy.58, f32[128,2]{1,0:T(8,128)S(1)} %copy.64), kind=kLoop, calls=%fused_computation.9 | loop fusion | flops 5505024 | bytes 9438720 | tf_op jit(solution)/shard_map/reduce_sum | solution.py:122
  405.6 1.5 collective-permute-start
  407.1 35.3 %collective-permute-done = bf16[1,128,6144]{2,1,0:T(8,128)(2,1)S(1)} collective-permute-done((bf16[1,128,6144]{2,1,0:T(8,128)(2,1)S(1)}, bf16[1,128,6144]{2,1,0:T(8,128)(2,1)S(1)}, u32[]{:S(2)}, u32[]{:S(2)}) %collective-permute-start) | collective-permute-done | bytes 1572896 | tf_op jit(solution)/shard_map/ppermute | solution.py:31
  (64 shorter events, 9.5 us)
Async XLA Ops:
  6.5 3.2 copy-start.7
  6.5 231.2 %all-gather.6.cloned.1.call-start = ((), (), s32[]{:S(2)}) async-start(), calls=%async_computation.1 | async-start | bytes 28311552 | tf_op jit(solution)/shard_map/all_gather | solution.py:17
  10.1 1.2 copy-start.2
  15.0 0.7 copy-start.11
  15.0 289.9 %all-gather.8.cloned.1.call-start = ((), (), s32[]{:S(2)}) async-start(), calls=%async_computation.2 | async-start | bytes 1769472 | tf_op jit(solution)/shard_map/all_gather | solution.py:105
  17.9 15.1 %copy-start.1 = (bf16[16,8,48,128]{3,2,1,0:T(8,128)(2,1)}, bf16[16,8,48,128]{3,2,1,0:T(8,128)(2,1)S(1)}, u32[]{:S(2)}) copy-start(bf16[16,8,48,128]{3,2,1,0:T(8,128)(2,1)S(1)} %copy.68) | copy-start | bytes 4718596
  32.4 1.5 copy-start.3
  245.1 2.4 copy-start.8
  247.5 2.4 copy-start.4
  247.5 2.3 copy-start.9
  314.7 5.1 %copy-start.10 = (f32[1,128,2]{1,2,0:T(2,128)S(1)}, f32[1,128,2]{1,2,0:T(2,128)}, u32[]{:S(2)}) copy-start(f32[1,128,2]{1,2,0:T(2,128)} %param.21) | copy-start | bytes 3076
  314.7 5.4 %copy-start = (f32[128,48,128]{0,2,1:T(8,128)S(1)}, f32[128,48,128]{0,2,1:T(8,128)}, u32[]{:S(2)}) copy-start(f32[128,48,128]{0,2,1:T(8,128)} %get-tuple-element.65) | copy-start | bytes 9437188
  314.7 42.4 %all-to-all-start = ((bf16[8,16,6144]{2,1,0:T(8,128)(2,1)}), bf16[8,16,6144]{2,1,0:T(8,128)(2,1)}, u32[]{:S(2)}, u32[]{:S(2)}) async-start(bf16[8,16,6144]{2,1,0:T(8,128)(2,1)} %bitcast.103), calls=%async_computation | async-start | bytes 3145728 | tf_op jit(solution)/shard_map/all_to_all | solution.py:117
  372.0 32.9 %copy-start.5 = (bf16[1,128,6144]{2,1,0:T(8,128)(2,1)S(1)}, bf16[1,128,6144]{2,1,0:T(8,128)(2,1)}, u32[]{:S(2)}) copy-start(bf16[1,128,6144]{2,1,0:T(8,128)(2,1)} %param.13) | copy-start | bytes 4718596
  372.0 32.9 %copy-start.6 = (f32[1,128,6144]{2,1,0:T(8,128)S(1)}, f32[1,128,6144]{2,1,0:T(8,128)}, u32[]{:S(2)}) copy-start(f32[1,128,6144]{2,1,0:T(8,128)} %copy.57) | copy-start | bytes 9437188
  405.6 36.8 %collective-permute-start = (bf16[1,128,6144]{2,1,0:T(8,128)(2,1)S(1)}, bf16[1,128,6144]{2,1,0:T(8,128)(2,1)S(1)}, u32[]{:S(2)}, u32[]{:S(2)}) collective-permute-start(bf16[1,128,6144]{2,1,0:T(8,128)(2,1)S(1)} %fusion.8), channel_id=1, source_target_pairs={{0,8},{8,16},{16,24},{24,0},{1,9},{9,17},{17,25},{25,1},{2,10},{10... | collective-permute-start | bytes 4718600 | tf_op jit(solution)/shard_map/ppermute | solution.py:31
Sparse Core Ops, SparseCore 0:
  15.1 222.5 all-gather.5
  264.2 40.6 all-gather.7
where the time goes:
time: 451 us; the launch traced here: 450 us
  waiting for transfers between devices  309 us (69%)
  other arithmetic  40.5 us (9%)
  local copies, waits for them, and re-layouts  39.8 us (9%)
  matrix products  27.4 us (6%)
  between operations  13.7 us (3%)
  blocking collectives  13.5 us (3%)
  starting transfers between devices  6.34 us (1%)
    all_gather x1, waiting for transfers between devices, prefix_2(): gathered = jax.tree.map(lambda a: lax.all_gather(a, axis), part)  198 us
    all_gather x1, waiting for transfers between devices, local(): lax.all_gather(outbox[None], 'ctx', axis=0, tiled=True)  40.8 us
    ppermute x1, waiting for transfers between devices, passed_along(): return lax.ppermute(value, axis, pairs)  35.3 us
    all_to_all x1, waiting for transfers between devices, local(): lax.all_to_all(partial_value, 'ctx', split_axis=0, concat_axis=0, tiled=T...  34.6 us
    reduce_sum x1, other arithmetic, local(): mixed = picked.reshape(length, 2, D).sum(axis=1)  32.9 us
    all_gather x1, blocking collectives, prefix_2(): gathered = jax.tree.map(lambda a: lax.all_gather(a, axis), part)  13.5 us
    gather x2, local copies, waits for them, and re-layouts, local(): picked = jnp.take(summed, jnp.clip(target, 0, flying * CAP_SRC - 1), axis=0)  13.3 us
    dot_general x1, matrix products, local(): jnp.dot(hidden, down_local, preferred_element_type=jnp.float32)  9.77 us
  transfers between devices with their start and end apart: 4, of which 4 were waited for; matrix products, arithmetic and copies ran while one was open for 3% of the time, Pallas kernels for 0%

commit v1 on v0

--- a/solution.py
+++ b/solution.py
@@ -10,6 +10,28 @@
 SHARDS = 8
 CAP_SRC = 16
 HIGH = lax.Precision.HIGHEST
+
+
+def joined_along(pieces, dim):
+    lengths = list(pieces.shape[1:])
+    lengths[dim] *= pieces.shape[0]
+    return jnp.moveaxis(pieces, 0, dim).reshape(lengths)
+
+
+def doubled_2(array, axis):
+    size = lax.axis_size(axis)
+    blocks = array[None]
+    for level in range(size.bit_length() - 1):
+        apart = 1 << level
+        other = lax.ppermute(blocks, axis, [(i, i ^ apart) for i in range(size)])
+        both = jnp.stack([blocks, other])
+        upper = lax.axis_index(axis) >> level & 1
+        blocks = jnp.where(upper == 0, both, both[::-1]).reshape(-1, *array.shape)
+    return blocks
+
+
+def collect(x, axis, dim):
+    return joined_along(doubled_2(x, axis), dim)
 
 
 def prefix_2(part, axis, combine, identity):
@@ -101,9 +123,7 @@
     outbox = outbox.reshape(flying, CAP_SRC, D)
     up_local = w_up[0]
     down_local = w_down[0]
-    mine = lax.dynamic_index_in_dim(
-        lax.all_gather(outbox[None], "ctx", axis=0, tiled=True), my_expert, 1, False
-    )
+    mine = lax.dynamic_index_in_dim(collect(outbox[None], "ctx", 0), my_expert, 1, False)
     count = mine.shape[0]
     hidden = jax.nn.gelu(
         jnp.dot(mine.reshape(count * CAP_SRC, D), up_local, preferred_element_type=jnp.float32),

time: 451 us -> 474 us (1.051)
  starting transfers between devices: 6.34 us -> 25.5 us
    ppermute x0 -> x3, waiting for transfers between devices: none -> 45.1 us  [doubled_2(): other = lax.ppermute(blocks, axis, [(i, i ^ apart) for i in range(size)])]
    all_gather x1 -> x0, waiting for transfers between devices: 40.8 us -> none  [local(): lax.all_gather(outbox[None], 'ctx', axis=0, tiled=True)]
    ppermute x0 -> x3, starting transfers between devices: none -> 18.7 us  [doubled_2(): other = lax.ppermute(blocks, axis, [(i, i ^ apart) for i in range(size)])]
  transfers between devices with their start and end apart: 4 -> 6, of which waited for: 4 -> 6; matrix products, arithmetic and copies ran while one was open for 3% -> 3% of each run, Pallas kernels for 0% -> 0%
where the time goes in v1:
time: 474 us
  waiting for transfers between devices  313 us (66%)
  other arithmetic  41.3 us (9%)
  local copies, waits for them, and re-layouts  39.9 us (8%)
  matrix products  26.3 us (6%)
  starting transfers between devices  25.5 us (5%)
  between operations  13.7 us (3%)
  blocking collectives  13.5 us (3%)
    all_gather x1, waiting for transfers between devices, prefix_2(): gathered = jax.tree.map(lambda a: lax.all_gather(a, axis), part)  198 us
    ppermute x3, waiting for transfers between devices, doubled_2(): other = lax.ppermute(blocks, axis, [(i, i ^ apart) for i in range(size)])  45.1 us
    ppermute x1, waiting for transfers between devices, passed_along(): return lax.ppermute(value, axis, pairs)  35.1 us
    all_to_all x1, waiting for transfers between devices, local(): lax.all_to_all(partial_value, 'ctx', split_axis=0, concat_axis=0, tiled=T...  34.9 us
    reduce_sum x1, other arithmetic, local(): mixed = picked.reshape(length, 2, D).sum(axis=1)  32.9 us
    ppermute x3, starting transfers between devices, doubled_2(): other = lax.ppermute(blocks, axis, [(i, i ^ apart) for i in range(size)])  18.7 us
    all_gather x1, blocking collectives, prefix_2(): gathered = jax.tree.map(lambda a: lax.all_gather(a, axis), part)  13.5 us
    gather x2, local copies, waits for them, and re-layouts, local(): picked = jnp.take(summed, jnp.clip(target, 0, flying * CAP_SRC - 1), axis=0)  13.3 us
  transfers between devices with their start and end apart: 6, of which 6 were waited for; matrix products, arithmetic and copies ran while one was open for 3% of the time, Pallas kernels for 0%

profile of v1, /device:TPU:0, one launch (start us, length us, event | category | flops | bytes accessed | tf_op | source)
XLA Modules:
  0.0 473.6 jit_solution(9470103437876923016)
XLA Ops:
  7.8 1.9 copy.66
  11.3 3.6 fusion.11
  18.8 13.5 %all-gather.1 = f32[8,1,48]{2,1,0:T(1,128)S(1)} all-gather(f32[1,1,48]{2,1,0:T(1,128)S(1)} %get-tuple-element.65), channel_id=1, replica_groups=mesh['section'=4,'ctx'=8] {'ctx'}, dimensions={0}, use_global_device_ids=true | all-gather | bytes 1728 | tf_op jit(solution)/shard_map/all_gather | solution.py:39
  34.0 5.5 %fusion.14 = f32[48,128,128]{1,2,0:T(8,128)} fusion(f32[48,128,128]{2,1,0:T(8,128)S(1)} %fusion.27, f32[48,128]{1,0:T(8,128)S(1)} %copy.48, pred[128,128]{1,0:T(8,128)(4,1)S(1)} %iota_compare_fusion, bf16[128,48,128]{2,1,0:T(8,128)(2,1)S(1)} %bitcast.113), kind=kOutput, calls=%fused_computation.24 | convolution fusion | flops 1210318848 | bytes 7905280 | tf_op jit(solution)/shard_map/hts,shd->thd/dot_general | solution.py:97
  39.4 198.3 %all-gather.4.cloned.1.call-done = f32[384,128,128]{2,1,0:T(8,128)} async-done(((f32[48,128,128]{2,1,0:T(8,128)}), f32[384,128,128]{2,1,0:T(8,128)}) %all-gather.4.cloned.1.call-update) | async-done | bytes 25165840 | tf_op jit(solution)/shard_map/all_gather | solution.py:39
  238.3 6.8 %multiply_reduce_fusion.2 = (f32[128]{0:T(128)S(1)}, f32[128,48,128]{0,2,1:T(8,128)}) fusion(f32[48,128,128]{2,1,0:T(8,128)S(1)} %get-tuple-element.49, bf16[128,48,128]{2,1,0:T(8,128)(2,1)} %bitcast.109, f32[128,48]{0,1:T(8,128)S(1)} %copy.51, f32[48,128,128]{1,2,0:T(8,128)} %fusion.14), kind=kOutput, calls=%fused_computation.20 | convolution fusion | flops 1211105152 | bytes 11035136 | tf_op jit(solution)/shard_map/thd,hde->the/dot_general | solution.py:105
  245.1 2.4 copy.63
  247.5 2.3 multiply_reduce_fusion.1
  249.8 1.9 multiply_convert_fusion
  251.7 5.0 %broadcast_in_dim.63 = bf16[128,2,6144]{2,1,0:T(2,128)(2,1)} broadcast(bf16[128,6144]{1,0:T(8,128)(2,1)} %multiply_convert_fusion), dimensions={0,2} | broadcast | bytes 4718592 | tf_op jit(solution)/shard_map/broadcast_in_dim | solution.py:121
  256.7 6.2 %reshape.253 = bf16[256,6144]{1,0:T(8,128)(2,1)S(1)} reshape(bf16[128,2,6144]{2,1,0:T(2,128)(2,1)} %broadcast_in_dim.63) | data formatting | bytes 6291456 | tf_op jit(solution)/shard_map/reshape | solution.py:121
  263.4 2.8 collective-permute-start
  267.4 3.6 collective-permute-start.1
  270.9 9.7 %collective-permute-done.1 = bf16[2,1,1,16,6144]{4,3,0,2,1:T(8,128)(2,1)S(1)} collective-permute-done((bf16[2,1,1,16,6144]{4,3,0,2,1:T(8,128)(2,1)S(1)}, bf16[2,1,1,16,6144]{4,3,0,2,1:T(8,128)(2,1)S(1)}, u32[]{:S(2)}, u32[]{:S(2)}) %collective-permute-start.1) | collective-permute-done | bytes 393248 | tf_op jit(solution)/shard_map/ppermute | solution.py:26
  280.8 12.3 %collective-permute-start.2 = (bf16[4,1,1,16,6144]{4,3,0,2,1:T(8,128)(2,1)S(1)}, bf16[4,1,1,16,6144]{4,3,0,2,1:T(8,128)(2,1)S(1)}, u32[]{:S(2)}, u32[]{:S(2)}) collective-permute-start(bf16[4,1,1,16,6144]{4,3,0,2,1:T(8,128)(2,1)S(1)} %bitcast.117), channel_id=1, source_target_pairs={{0,4},{1,5},{2,6},{3,7},{4,0},{5,1},{6,2},{7,3},{8,12},{9,13},{10,... | collective-permute-start | bytes 2359304 | tf_op jit(solution)/shard_map/ppermute | solution.py:26
  293.1 34.4 %collective-permute-done.2 = bf16[4,1,1,16,6144]{4,3,0,2,1:T(8,128)(2,1)S(1)} collective-permute-done((bf16[4,1,1,16,6144]{4,3,0,2,1:T(8,128)(2,1)S(1)}, bf16[4,1,1,16,6144]{4,3,0,2,1:T(8,128)(2,1)S(1)}, u32[]{:S(2)}, u32[]{:S(2)}) %collective-permute-start.2) | collective-permute-done | bytes 786464 | tf_op jit(solution)/shard_map/ppermute | solution.py:26
  328.0 9.3 %fusion.4 = bf16[128,6144]{1,0:T(8,128)(2,1)} fusion(bf16[1,640,6144]{2,1,0:T(8,128)(2,1)} %param.23, bf16[128,6144]{1,0:T(8,128)(2,1)S(1)} %bitcast.116, bf16[1,6144,640]{2,1,0:T(8,128)(2,1)} %param.22), kind=kOutput, calls=%fused_computation.7 | convolution fusion | flops 2014789632 | bytes 18874368 | tf_op jit(solution)/shard_map/dot_general | solution.py:133
  337.3 5.1 %all-to-all-start = ((bf16[8,16,6144]{2,1,0:T(8,128)(2,1)}), bf16[8,16,6144]{2,1,0:T(8,128)(2,1)}, u32[]{:S(2)}, u32[]{:S(2)}) async-start(bf16[8,16,6144]{2,1,0:T(8,128)(2,1)} %bitcast.115), calls=%async_computation | async-start | bytes 3145728 | tf_op jit(solution)/shard_map/all_to_all | solution.py:137
  343.0 2.4 copy.57
  345.4 34.9 %all-to-all-done = bf16[8,16,6144]{2,1,0:T(8,128)(2,1)} async-done(((bf16[8,16,6144]{2,1,0:T(8,128)(2,1)}), bf16[8,16,6144]{2,1,0:T(8,128)(2,1)}, u32[]{:S(2)}, u32[]{:S(2)}) %all-to-all-start) | async-done | bytes 1572896 | tf_op jit(solution)/shard_map/all_to_all | solution.py:137
  381.9 5.1 %gather_fusion = f32[256,6144]{1,0:T(8,128)} fusion(f32[16,6144]{1,0:T(8,128)S(1)} %convert_reduce_fusion, s32[1024]{0:T(1024)S(1)} %pad_clamp_fusion), kind=kCustom, calls=%fused_computation | custom fusion | bytes 12583936 | tf_op jit(solution)/shard_map/jit(_take)/gather | solution.py:140
  387.1 8.1 %gather.7 = f32[128,2,6144]{2,1,0:T(2,128)} reshape(f32[256,6144]{1,0:T(8,128)} %gather_fusion) | data formatting | bytes 12582912 | tf_op jit(solution)/shard_map/jit(_take)/gather | solution.py:140
  395.2 32.9 %multiply_reduce_fusion = f32[128,6144]{1,0:T(8,128)S(1)} fusion(f32[128,2,6144]{2,1,0:T(2,128)} %gather.7, pred[128,2]{1,0:T(8,128)(4,1)S(1)} %compare_and_fusion, pred[128,2]{1,0:T(8,128)(4,1)S(1)} %copy.58, f32[128,2]{1,0:T(8,128)S(1)} %copy.64), kind=kLoop, calls=%fused_computation.9 | loop fusion | flops 5505024 | bytes 9438720 | tf_op jit(solution)/shard_map/reduce_sum | solution.py:142
  430.6 35.1 %collective-permute-done.3 = bf16[1,128,6144]{2,1,0:T(8,128)(2,1)S(1)} collective-permute-done((bf16[1,128,6144]{2,1,0:T(8,128)(2,1)S(1)}, bf16[1,128,6144]{2,1,0:T(8,128)(2,1)S(1)}, u32[]{:S(2)}, u32[]{:S(2)}) %collective-permute-start.3) | collective-permute-done | bytes 1572896 | tf_op jit(solution)/shard_map/ppermute | solution.py:53
  (73 shorter events, 17.1 us)
Async XLA Ops:
  6.5 3.2 copy-start.7
  6.5 231.2 %all-gather.4.cloned.1.call-start = ((), (), s32[]{:S(2)}) async-start(), calls=%async_computation.1 | async-start | bytes 28311552 | tf_op jit(solution)/shard_map/all_gather | solution.py:39
  10.1 1.2 copy-start.2
  15.0 0.7 copy-start.11
  17.9 15.1 %copy-start.1 = (bf16[16,8,48,128]{3,2,1,0:T(8,128)(2,1)}, bf16[16,8,48,128]{3,2,1,0:T(8,128)(2,1)S(1)}, u32[]{:S(2)}) copy-start(bf16[16,8,48,128]{3,2,1,0:T(8,128)(2,1)S(1)} %copy.68) | copy-start | bytes 4718596
  32.4 1.5 copy-start.3
  245.1 2.4 copy-start.8
  247.5 2.4 copy-start.4
  247.5 2.3 copy-start.9
  263.4 3.9 collective-permute-start
  267.4 13.2 %collective-permute-start.1 = (bf16[2,1,1,16,6144]{4,3,0,2,1:T(8,128)(2,1)S(1)}, bf16[2,1,1,16,6144]{4,3,0,2,1:T(8,128)(2,1)S(1)}, u32[]{:S(2)}, u32[]{:S(2)}) collective-permute-start(bf16[2,1,1,16,6144]{4,3,0,2,1:T(8,128)(2,1)S(1)} %get-tuple-element.61), channel_id=1, source_target_pairs={{0,2},{1,3},{2,0},{3,1},{4,6},{5,7},{6,4},{7,5},{8,10},{9,11},{10,... | collective-permute-start | bytes 1179656 | tf_op jit(solution)/shard_map/ppermute | solution.py:26
  280.8 46.7 %collective-permute-start.2 = (bf16[4,1,1,16,6144]{4,3,0,2,1:T(8,128)(2,1)S(1)}, bf16[4,1,1,16,6144]{4,3,0,2,1:T(8,128)(2,1)S(1)}, u32[]{:S(2)}, u32[]{:S(2)}) collective-permute-start(bf16[4,1,1,16,6144]{4,3,0,2,1:T(8,128)(2,1)S(1)} %bitcast.117), channel_id=1, source_target_pairs={{0,4},{1,5},{2,6},{3,7},{4,0},{5,1},{6,2},{7,3},{8,12},{9,13},{10,... | collective-permute-start | bytes 2359304 | tf_op jit(solution)/shard_map/ppermute | solution.py:26
  337.3 5.4 %copy-start.10 = (f32[1,128,2]{1,2,0:T(2,128)S(1)}, f32[1,128,2]{1,2,0:T(2,128)}, u32[]{:S(2)}) copy-start(f32[1,128,2]{1,2,0:T(2,128)} %param.21) | copy-start | bytes 3076
  337.3 5.7 %copy-start = (f32[128,48,128]{0,2,1:T(8,128)S(1)}, f32[128,48,128]{0,2,1:T(8,128)}, u32[]{:S(2)}) copy-start(f32[128,48,128]{0,2,1:T(8,128)} %get-tuple-element.67) | copy-start | bytes 9437188
  337.3 43.0 %all-to-all-start = ((bf16[8,16,6144]{2,1,0:T(8,128)(2,1)}), bf16[8,16,6144]{2,1,0:T(8,128)(2,1)}, u32[]{:S(2)}, u32[]{:S(2)}) async-start(bf16[8,16,6144]{2,1,0:T(8,128)(2,1)} %bitcast.115), calls=%async_computation | async-start | bytes 3145728 | tf_op jit(solution)/shard_map/all_to_all | solution.py:137
  395.2 32.9 %copy-start.5 = (bf16[1,128,6144]{2,1,0:T(8,128)(2,1)S(1)}, bf16[1,128,6144]{2,1,0:T(8,128)(2,1)}, u32[]{:S(2)}) copy-start(bf16[1,128,6144]{2,1,0:T(8,128)(2,1)} %param.13) | copy-start | bytes 4718596
  395.2 32.9 %copy-start.6 = (f32[1,128,6144]{2,1,0:T(8,128)S(1)}, f32[1,128,6144]{2,1,0:T(8,128)}, u32[]{:S(2)}) copy-start(f32[1,128,6144]{2,1,0:T(8,128)} %copy.57) | copy-start | bytes 9437188
  428.8 36.8 %collective-permute-start.3 = (bf16[1,128,6144]{2,1,0:T(8,128)(2,1)S(1)}, bf16[1,128,6144]{2,1,0:T(8,128)(2,1)S(1)}, u32[]{:S(2)}, u32[]{:S(2)}) collective-permute-start(bf16[1,128,6144]{2,1,0:T(8,128)(2,1)S(1)} %fusion.8), channel_id=1, source_target_pairs={{0,8},{8,16},{16,24},{24,0},{1,9},{9,17},{17,25},{25,1},{2,10},{10... | collective-permute-start | bytes 4718600 | tf_op jit(solution)/shard_map/ppermute | solution.py:53
Sparse Core Ops, SparseCore 0:
  15.1 222.5 all-gather.3
